TPU v7x, 256 devices: a whole 4x4x8 slice. The times are simulated.
256 devices in a mesh: row: 16 (over z, core), col: 8 (over x_hi, y), lrn: 2 (over x_lo).
Axes of the slice: x: 4 (x_hi: 2, x_lo: 2; x = x_hi * 2 + x_lo), y: 4, z: 8, core: 2. Of those that a mesh axis runs over, the one named last changes fastest.
Arguments:
- responses: int32 [4096, 16384], P('lrn', ('row', 'col')), may hold values 0 or 1
- observed: int32 [4096, 16384], P('lrn', ('row', 'col')), may hold values from 0 to 1, as said below
- qmatrix: int32 [16384, 8], P(('row', 'col')), may hold values from 0 to 1
- guess: float32 [16384], P(('row', 'col')), may hold values from 0.05 to 0.35
- slip: float32 [16384], P(('row', 'col')), may hold values from 0.05 to 0.35
Outputs:
- q3_scaled: float32 [16384, 16384], P('row', ('col', 'lrn'))
Inputs may be any that keep to these rules, and one draw needn't show every extreme that they name: Some items have no observed response from any learner.
All inputs are finite; a program needn't handle non-finite values. No bound on the sum of `responses` on one device may be relied on, other than what follows from the above.
Results may differ from a plain program's by a relative error of at most 0.008.
Values may be sent and summed in bfloat16 or wider, within the bound.
No kernel may reach another device: no remote copies, remote signals or barrier semaphores. Data moves between devices by JAX's collectives and lax.ppermute only.
A program may use at most 128 MiB of HBM per device.

v0:
```python
import jax
import jax.numpy as jnp
from jax import lax
from jax.sharding import PartitionSpec as P

ATTRS = 8
PROFILES = 256


def spread(x, axis, root):
    mine = lax.axis_index(axis) == root
    return lax.psum(jnp.where(mine, x, jnp.zeros_like(x)), axis)


def success(qmatrix, guess, slip):
    codes = jnp.arange(PROFILES, dtype=jnp.int32)
    powers = jnp.arange(ATTRS, dtype=jnp.int32)
    bits = (codes[None, :] >> powers[:, None] & 1).astype(jnp.float32)
    lacking = jnp.dot(qmatrix.astype(jnp.float32), 1.0 - bits, precision=lax.Precision.HIGHEST)
    return jnp.where(lacking == 0.0, 1.0 - slip[:, None], guess[:, None])


def learner_product(left, right):
    return lax.dot_general(
        left, right, (((0,), (0,)), ((), ())), preferred_element_type=jnp.float32
    )


def shards(responses, observed, qmatrix, guess, slip):
    prob = success(qmatrix, guess, slip)
    answered = responses.astype(jnp.float32)
    seen = observed.astype(jnp.float32)
    partial_value = jnp.dot(seen * answered, jnp.log(prob), precision=lax.Precision.HIGHEST)
    partial_value = partial_value + jnp.dot(
        seen * (1.0 - answered), jnp.log(1.0 - prob), precision=lax.Precision.HIGHEST
    )
    loglik = lax.psum(partial_value, ("row", "col"))
    posterior = jax.nn.softmax(loglik, axis=1).astype(jnp.bfloat16)
    expected = jnp.dot(posterior, prob.astype(jnp.bfloat16).T, preferred_element_type=jnp.float32)
    resid = seen * (answered - expected)
    count, total, square = lax.psum(
        (jnp.sum(seen, axis=0), jnp.sum(resid, axis=0), jnp.sum(resid * resid, axis=0)), "lrn"
    )
    count = jnp.maximum(count, 1.0)
    mean = total / count
    var = square / count - mean * mean
    zres = (seen * (resid - mean) * lax.rsqrt(var + 1e-06) * lax.rsqrt(count)).astype(jnp.bfloat16)
    panel = lax.all_gather(zres, "col", axis=1, tiled=True)
    learner_total = zres.shape[0] * lax.axis_size("lrn")
    whole_panel = lax.all_gather(panel, "lrn", axis=0, tiled=True)
    repeats = lax.axis_size("row") // (lax.axis_size("col") * lax.axis_size("lrn"))
    tile_index = lax.axis_index("col") * lax.axis_size("lrn") + lax.axis_index("lrn")
    pieces = spread(whole_panel, "row", tile_index * repeats + 0)
    gram = learner_product(whole_panel, pieces)
    return gram * jnp.sqrt(jnp.float32(learner_total))


def solution(mesh):
    placed = (
        P("lrn", ("row", "col")),
        P("lrn", ("row", "col")),
        P(("row", "col"), None),
        P(("row", "col")),
        P(("row", "col")),
    )
    return jax.shard_map(
        shards, mesh=mesh, in_specs=placed, out_specs=P("row", ("col", "lrn")), check_vma=False
    )
```

profile of v0, /device:TPU:2, one launch (start us, length us, event | category | flops | bytes accessed | tf_op | source)
XLA Modules:
  0.0 1652.2 jit_solution(6100974589586948307)
XLA Ops:
  6.5 0.0 all-reduce.4.cloned.1.call-start
  6.5 0.8 broadcast_subtract_fusion
  7.3 1.1 fusion
  8.4 0.0 copy-start.2
  8.5 3.4 fusion.3
  11.9 0.0 copy-done
  11.9 3.2 convolution_add_fusion
  15.1 0.0 all-reduce.4.cloned.1.call-update
  15.1 0.0 all-gather.3.cloned.1.call-start
  15.1 1279.9 %all-reduce.4.cloned.1.call-done = f32[2048,256]{1,0:T(8,128)} async-done(((f32[2048,256]{1,0:T(8,128)}), f32[2048,256]{1,0:T(8,128)}) %all-reduce.4.cloned.1.call-update) | async-done | bytes 2097168 | tf_op jit(solution)/shard_map/psum | solution.py:37
  1295.0 3.9 online-softmax
  1298.9 1.5 multiply_reduce_fusion
  1300.4 4.9 all-reduce
  1305.4 1.0 multiply_convert_fusion
  1306.4 0.0 all-gather.3.cloned.1.call-update
  1306.4 0.0 all-gather.5.cloned.1.call-start
  1306.5 72.4 %all-gather.3.cloned.1.call-done = bf16[2048,1024]{1,0:T(8,128)(2,1)} async-done(((bf16[2048,128]{1,0:T(8,128)(2,1)}), bf16[2048,1024]{1,0:T(8,128)(2,1)}) %all-gather.3.cloned.1.call-update) | async-done | bytes 4194320 | tf_op jit(solution)/shard_map/all_gather | solution.py:48
  1378.8 0.0 all-gather.5.cloned.1.call-update
  1378.9 0.0 all-reduce.6.cloned.1.call-start
  1378.9 108.7 %all-gather.5.cloned.1.call-done = bf16[4096,1024]{1,0:T(8,128)(2,1)} async-done(((bf16[2048,1024]{1,0:T(8,128)(2,1)}), bf16[4096,1024]{1,0:T(8,128)(2,1)}) %all-gather.5.cloned.1.call-update) | async-done | bytes 8388624 | tf_op jit(solution)/shard_map/all_gather | solution.py:50
  1487.6 3.8 broadcast_select_fusion
  1491.4 0.0 all-reduce.6.cloned.1.call-update
  1491.4 139.2 %all-reduce.6.cloned.1.call-done = bf16[4096,1024]{1,0:T(8,128)(2,1)} async-done(((bf16[4096,1024]{1,0:T(8,128)(2,1)}), bf16[4096,1024]{1,0:T(8,128)(2,1)}) %all-reduce.6.cloned.1.call-update) | async-done | bytes 8388624 | tf_op jit(solution)/shard_map/psum | solution.py:12
  1630.6 15.0 convolution_multiply_fusion
  (5 shorter events, 0.0 us)
Async XLA Ops:
  6.5 5.4 copy-start
  6.5 5.4 copy-start.1
  6.5 1288.5 %all-reduce.4.cloned.1.call-start = ((), (), s32[]{:S(2)}) async-start(), calls=%async_computation | async-start | bytes 4194304 | tf_op jit(solution)/shard_map/psum | solution.py:37
  8.4 6.6 copy-start.2
  15.1 1363.7 %all-gather.3.cloned.1.call-start = ((), (), s32[]{:S(2)}) async-start(), calls=%async_computation.1 | async-start | bytes 4718592 | tf_op jit(solution)/shard_map/all_gather | solution.py:48
  1306.4 181.2 %all-gather.5.cloned.1.call-start = ((), (), s32[]{:S(2)}) async-start(), calls=%async_computation.2 | async-start | bytes 12582912 | tf_op jit(solution)/shard_map/all_gather | solution.py:50
  1378.9 251.8 %all-reduce.6.cloned.1.call-start = ((), (), s32[]{:S(2)}) async-start(), calls=%async_computation.3 | async-start | bytes 16777216 | tf_op jit(solution)/shard_map/psum | solution.py:12
Sparse Core Ops, SparseCore 0:
  15.2 1279.7 all-reduce.3
  1306.5 72.2 all-gather.2
  1380.8 106.7 all-gather.4
  1491.5 139.0 all-reduce.5
where the time goes:
time: 1650 us
  waiting for transfers between devices  1600 us (97%)
  matrix products  22.7 us (1%)
    psum x1, waiting for transfers between devices, shards(): loglik = lax.psum(partial_value, ('row', 'col'))  1280 us
    psum x1, waiting for transfers between devices, spread(): return lax.psum(jnp.where(mine, x, jnp.zeros_like(x)), axis)  139 us
    all_gather x1, waiting for transfers between devices, shards(): whole_panel = lax.all_gather(panel, 'lrn', axis=0, tiled=True)  109 us
    all_gather x1, waiting for transfers between devices, shards(): panel = lax.all_gather(zres, 'col', axis=1, tiled=True)  72.4 us
  transfers between devices with their start and end apart: 4, of which 4 were waited for; matrix products, arithmetic and copies ran while one was open for 0% of the time, Pallas kernels for 0%

commit v1 on v0

--- a/solution.py
+++ b/solution.py
@@ -34,7 +34,7 @@
     partial_value = partial_value + jnp.dot(
         seen * (1.0 - answered), jnp.log(1.0 - prob), precision=lax.Precision.HIGHEST
     )
-    loglik = lax.psum(partial_value, ("row", "col"))
+    loglik = lax.psum(lax.psum(partial_value, "row"), "col")
     posterior = jax.nn.softmax(loglik, axis=1).astype(jnp.bfloat16)
     expected = jnp.dot(posterior, prob.astype(jnp.bfloat16).T, preferred_element_type=jnp.float32)
     resid = seen * (answered - expected)

time: 1650 us -> 595 us (0.36)
  waiting for transfers between devices: 1600 us -> 543 us
    psum x1 -> x2, waiting for transfers between devices: 1280 us -> 217 us  [shards(): loglik = lax.psum(lax.psum(partial_value, 'row'), 'col')]
  transfers between devices with their start and end apart: 4 -> 5, of which waited for: 4 -> 5; matrix products, arithmetic and copies ran while one was open for 0% -> 0% of each run, Pallas kernels for 0% -> 0%
where the time goes in v1:
time: 595 us
  waiting for transfers between devices  543 us (91%)
  matrix products  22.7 us (4%)
  between operations  13.2 us (2%)
  other arithmetic  7.1 us (1%)
    psum x2, waiting for transfers between devices, shards(): loglik = lax.psum(lax.psum(partial_value, 'row'), 'col')  217 us
    psum x1, waiting for transfers between devices, spread(): return lax.psum(jnp.where(mine, x, jnp.zeros_like(x)), axis)  139 us
    all_gather x1, waiting for transfers between devices, shards(): whole_panel = lax.all_gather(panel, 'lrn', axis=0, tiled=True)  108 us
    all_gather x1, waiting for transfers between devices, shards(): panel = lax.all_gather(zres, 'col', axis=1, tiled=True)  77.5 us
    dot_general x1, matrix products, learner_product(): lax.dot_general(left, right, (((0,), (0,)), ((), ())), preferred_element_...  15 us
  transfers between devices with their start and end apart: 5, of which 5 were waited for; matrix products, arithmetic and copies ran while one was open for 0% of the time, Pallas kernels for 0%

profile of v1, /device:TPU:2, one launch (start us, length us, event | category | flops | bytes accessed | tf_op | source)
XLA Modules:
  0.0 594.7 jit_solution(11264202702036551961)
XLA Ops:
  6.5 0.8 broadcast_subtract_fusion
  7.3 1.1 fusion
  8.5 3.4 fusion.3
  11.9 3.2 convolution_add_fusion
  15.1 0.0 all-reduce.5.cloned.1.call-update
  15.1 0.0 all-reduce.7.cloned.1.call-start
  15.1 118.0 %all-reduce.5.cloned.1.call-done = f32[2048,256]{1,0:T(8,128)} async-done(((f32[2048,256]{1,0:T(8,128)}), f32[2048,256]{1,0:T(8,128)}) %all-reduce.5.cloned.1.call-update) | async-done | bytes 2097168 | tf_op jit(solution)/shard_map/psum | solution.py:37
  133.2 0.0 all-reduce.7.cloned.1.call-update
  133.2 0.0 all-gather.3.cloned.1.call-start
  133.3 99.4 %all-reduce.7.cloned.1.call-done = f32[2048,256]{1,0:T(8,128)} async-done(((f32[2048,256]{1,0:T(8,128)}), f32[2048,256]{1,0:T(8,128)}) %all-reduce.7.cloned.1.call-update) | async-done | bytes 2097168 | tf_op jit(solution)/shard_map/psum | solution.py:37
  232.6 3.9 online-softmax
  236.5 1.5 multiply_reduce_fusion
  238.1 4.9 all-reduce
  243.0 1.0 multiply_convert_fusion
  244.0 0.0 all-gather.3.cloned.1.call-update
  244.1 0.0 all-gather.5.cloned.1.call-start
  244.1 77.5 %all-gather.3.cloned.1.call-done = bf16[2048,1024]{1,0:T(8,128)(2,1)} async-done(((bf16[2048,128]{1,0:T(8,128)(2,1)}), bf16[2048,1024]{1,0:T(8,128)(2,1)}) %all-gather.3.cloned.1.call-update) | async-done | bytes 4194320 | tf_op jit(solution)/shard_map/all_gather | solution.py:48
  321.6 0.0 all-gather.5.cloned.1.call-update
  321.6 0.0 all-reduce.9.cloned.1.call-start
  321.7 108.4 %all-gather.5.cloned.1.call-done = bf16[4096,1024]{1,0:T(8,128)(2,1)} async-done(((bf16[2048,1024]{1,0:T(8,128)(2,1)}), bf16[4096,1024]{1,0:T(8,128)(2,1)}) %all-gather.5.cloned.1.call-update) | async-done | bytes 8388624 | tf_op jit(solution)/shard_map/all_gather | solution.py:50
  430.1 3.8 broadcast_select_fusion
  433.8 0.0 all-reduce.9.cloned.1.call-update
  433.9 139.2 %all-reduce.9.cloned.1.call-done = bf16[4096,1024]{1,0:T(8,128)(2,1)} async-done(((bf16[4096,1024]{1,0:T(8,128)(2,1)}), bf16[4096,1024]{1,0:T(8,128)(2,1)}) %all-reduce.9.cloned.1.call-update) | async-done | bytes 8388624 | tf_op jit(solution)/shard_map/psum | solution.py:12
  573.1 15.0 %convolution_multiply_fusion = f32[1024,1024]{1,0:T(8,128)} fusion(bf16[4096,1024]{1,0:T(8,128)(2,1)} %all-gather.5.cloned.1.call-done, bf16[4096,1024]{1,0:T(8,128)(2,1)} %all-reduce.9.cloned.1.call-done), kind=kOutput, calls=%fused_computation.2 | convolution fusion | flops 8590983168 | bytes 20971520 | tf_op jit(solution)/shard_map/dot_general | solution.py:24
  (8 shorter events, 0.0 us)
Async XLA Ops:
  6.5 5.4 copy-start
  6.5 5.4 copy-start.1
  6.5 126.6 %all-reduce.5.cloned.1.call-start = ((), (), s32[]{:S(2)}) async-start(), calls=%async_computation | async-start | bytes 4194304 | tf_op jit(solution)/shard_map/psum | solution.py:37
  8.4 6.6 %copy-start.2 = (f32[256,128]{1,0:T(8,128)}, f32[256,128]{1,0:T(8,128)S(1)}, u32[]{:S(2)}) copy-start(f32[256,128]{1,0:T(8,128)S(1)} %fusion) | copy-start | bytes 393220
  15.1 217.6 %all-reduce.7.cloned.1.call-start = ((), (), s32[]{:S(2)}) async-start(), calls=%async_computation.1 | async-start | bytes 4194304 | tf_op jit(solution)/shard_map/psum | solution.py:37
  133.2 188.4 %all-gather.3.cloned.1.call-start = ((), (), s32[]{:S(2)}) async-start(), calls=%async_computation.2 | async-start | bytes 4718592 | tf_op jit(solution)/shard_map/all_gather | solution.py:48
  244.1 186.0 %all-gather.5.cloned.1.call-start = ((), (), s32[]{:S(2)}) async-start(), calls=%async_computation.3 | async-start | bytes 12582912 | tf_op jit(solution)/shard_map/all_gather | solution.py:50
  321.6 251.5 %all-reduce.9.cloned.1.call-start = ((), (), s32[]{:S(2)}) async-start(), calls=%async_computation.4 | async-start | bytes 16777216 | tf_op jit(solution)/shard_map/psum | solution.py:12
Sparse Core Ops, SparseCore 0:
  15.2 117.9 all-reduce.4
  135.8 96.7 all-reduce.6
  244.2 77.3 all-gather.2
  323.2 106.7 all-gather.4
  434.0 139.0 all-reduce.8
